TPU v7x, 512 devices: a whole 4x4x16 slice. The times are simulated.
512 devices in a mesh: dom: 32 (over x_hi, z), grp: 16 (over y, x_lo, core).
Axes of the slice: x: 4 (x_hi: 2, x_lo: 2; x = x_hi * 2 + x_lo), y: 4, z: 16, core: 2. Of those that a mesh axis runs over, the one named last changes fastest.
Arguments:
- adjoint_state: float32 [64, 16, 1024, 256], P('grp', None, 'dom'), may hold values from -6 to 6
- east_wind: float32 [16, 1024, 256], P(None, 'dom'), may hold values from -0.2 to 0.2
- north_wind: float32 [16, 1024, 256], P(None, 'dom'), may hold values from -0.2 to 0.2
- east_diff: float32 [16, 1024, 256], P(None, 'dom'), may hold values from 0.01 to 0.05
- north_diff: float32 [16, 1024, 256], P(None, 'dom'), may hold values from 0.01 to 0.05
- mass_flux: float32 [16, 1024, 256], P(None, 'dom'), may hold values from 0.05 to 0.45
- region_map: int32 [1024, 256], P('dom'), may hold values from 0 to 63
- cloud_top: int32 [1024, 256], P('dom'), may hold values from 1 to 15
Outputs:
- final_adjoint: float32 [64, 16, 1024, 256], P('grp', None, 'dom')
- flux_gradient: float32 [1024, 256], P('dom')
Inputs may be any that keep to these rules, and one draw needn't show every extreme that they name: `region_map`: tag k of the whole set of 64 tags belongs to region k.
All inputs are finite; a program needn't handle non-finite values.
Results may differ from a plain program's by a relative error of at most 0.00002.
Values sent between devices are 32-bit elements; how exact they have to be, the bound alone decides.
A program may use at most 64 MiB of HBM per device.

v0:
```python
import jax
import jax.numpy as jnp
from jax import lax
from jax.sharding import PartitionSpec as P

ITERS = 4


def passed_along(value, axis, by):
    size = lax.axis_size(axis)
    return lax.ppermute(value, axis, [(i, (i + by) % size) for i in range(size)])


def with_halo(cells, sides, width):
    for axis, dim in sides:
        count = lax.axis_size(axis)
        head = lax.slice_in_dim(cells, 0, width, axis=dim)
        tail = lax.slice_in_dim(cells, cells.shape[dim] - width, cells.shape[dim], axis=dim)
        cells = jnp.concatenate(
            [
                lax.ppermute(tail, axis, [(i, (i + 1) % count) for i in range(count)]),
                cells,
                lax.ppermute(head, axis, [((i + 1) % count, i) for i in range(count)]),
            ],
            axis=dim,
        )
    return cells


def local(
    adjoint_state, east_wind, north_wind, east_diff, north_diff, mass_flux, region_map, cloud_top
):
    tags, levels, cols, lats = adjoint_state.shape
    level_ids = lax.broadcasted_iota(jnp.int32, mass_flux.shape, 0)
    active = mass_flux * (level_ids < cloud_top[None]).astype(jnp.float32)
    stacked = jnp.stack([east_wind, east_diff, north_wind, north_diff, active])
    margin = 1
    edge = stacked[0:2, :, cols - 1 : cols]
    left_edge = passed_along(edge, "dom", 1)
    lower_rim = jnp.concatenate(
        [left_edge, jnp.zeros((3,) + left_edge.shape[1:], jnp.float32)], axis=0
    )
    padded = jnp.concatenate([lower_rim, stacked, jnp.zeros_like(lower_rim)], axis=2)
    wind_e = padded[0]
    diff_e = padded[1]
    wind_n = padded[2]
    diff_n = padded[3]
    updraft = padded[4]
    east_coef = jnp.maximum(wind_e, 0.0) + diff_e
    west_prime = jnp.maximum(-wind_e, 0.0) + diff_e
    row_ids = lax.broadcasted_iota(jnp.int32, wind_n.shape, 2)
    north_coef = (jnp.maximum(wind_n, 0.0) + diff_n) * (row_ids < lats - 1).astype(jnp.float32)
    south_prime = jnp.maximum(-wind_n, 0.0) + diff_n
    south_coef = jnp.concatenate(
        [jnp.zeros_like(south_prime[..., :1]), south_prime[..., :-1]], axis=-1
    )
    lam = adjoint_state
    accum = jnp.zeros((tags, cols, lats), jnp.float32)
    for round_step in range(ITERS // margin):
        current = with_halo(lam, (("dom", 2),), 1)
        center = current[:, :, 1 : 1 + cols]
        east = current[:, :, 2 : 2 + cols]
        west = current[:, :, 0:cols]
        coef_e = east_coef[:, margin : margin + cols]
        coef_w = west_prime[:, margin - 1 : margin - 1 + cols]
        coef_n = north_coef[:, margin : margin + cols]
        coef_s = south_coef[:, margin : margin + cols]
        lift = updraft[:, margin : margin + cols]
        north = jnp.concatenate([center[..., 1:], center[..., -1:]], axis=-1)
        south = jnp.concatenate([center[..., :1], center[..., :-1]], axis=-1)
        h = (
            center
            + coef_e * (east - center)
            + coef_w * (west - center)
            + coef_n * (north - center)
            + coef_s * (south - center)
        )
        above = jnp.concatenate([h[:, 1:], h[:, -1:]], axis=1)
        current = h + lift * (above - h)
        accum = accum + current[:, 0, 0:cols]
        lam = current
    tag_ids = lax.axis_index("grp") * tags + lax.broadcasted_iota(jnp.int32, (tags, cols, lats), 0)
    select = (region_map[None] == tag_ids).astype(jnp.float32)
    local_grad = jnp.sum(select * accum, axis=0)
    flux_gradient = lax.psum(local_grad, "grp")
    return (lam, flux_gradient)


def solution(mesh):
    return jax.shard_map(
        local,
        mesh=mesh,
        in_specs=(
            P("grp", None, "dom", None),
            P(None, "dom", None),
            P(None, "dom", None),
            P(None, "dom", None),
            P(None, "dom", None),
            P(None, "dom", None),
            P("dom", None),
            P("dom", None),
        ),
        out_specs=(P("grp", None, "dom", None), P("dom", None)),
        check_vma=False,
    )
```

profile of v0, /device:TPU:4, one launch (start us, length us, event | category | flops | bytes accessed | tf_op | source)
XLA Modules:
  0.0 145.7 jit_solution(17313663855327665156)
XLA Ops:
  0.6 1.2 pad_maximum_fusion.8
  1.8 3.8 %collective-permute-start = (f32[2,16,1,256]{3,2,1,0:T(1,128)S(1)}, f32[2,16,1,256]{3,2,1,0:T(1,128)S(1)}, u32[]{:S(2)}, u32[]{:S(2)}) collective-permute-start(f32[2,16,1,256]{3,2,1,0:T(1,128)S(1)} %pad_maximum_fusion.8), channel_id=1, source_target_pairs={{0,16},{16,32},{32,48},{48,64},{64,80},{80,96},{96,112},{112,128},... | collective-permute-start | bytes 98312 | tf_op jit(solution)/shard_map/ppermute | solution.py:11
  5.6 1.3 fusion.63
  6.9 9.4 %collective-permute-start.1 = (f32[4,16,1,256]{3,2,1,0:T(1,128)S(1)}, f32[4,16,1,256]{3,2,1,0:T(1,128)S(1)}, u32[]{:S(2)}, u32[]{:S(2)}) collective-permute-start(f32[4,16,1,256]{3,2,1,0:T(1,128)S(1)} %get-tuple-element.29), channel_id=1, source_target_pairs={{16,0},{32,16},{48,32},{64,48},{80,64},{96,80},{112,96},{128,112},... | collective-permute-start | bytes 196616 | tf_op jit(solution)/shard_map/ppermute | solution.py:23
  16.4 1.9 %collective-permute-start.2 = (f32[4,16,1,256]{3,2,1,0:T(1,128)S(1)}, f32[4,16,1,256]{3,2,1,0:T(1,128)S(1)}, u32[]{:S(2)}, u32[]{:S(2)}) collective-permute-start(f32[4,16,1,256]{3,2,1,0:T(1,128)S(1)} %get-tuple-element.30), channel_id=1, source_target_pairs={{0,16},{16,32},{32,48},{48,64},{64,80},{80,96},{96,112},{112,128},... | collective-permute-start | bytes 196616 | tf_op jit(solution)/shard_map/ppermute | solution.py:21
  18.3 1.9 %constant_dynamic-update-slice_fusion.1 = f32[5,16,32,256]{3,2,1,0:T(8,128)} fusion(f32[16,32,256]{2,1,0:T(8,128)} %param.9), kind=kLoop, calls=%fused_computation.90 | loop fusion | bytes 1048576
  20.2 2.8 %fusion.62 = (f32[4,16,32,255]{3,2,1,0:T(8,128)}, f32[4,16,32,255]{3,2,1,0:T(8,128)}) fusion(f32[4,16,32,256]{3,2,1,0:T(8,128)S(1)} %copy-done), kind=kLoop, calls=%fused_computation.103 | loop fusion | bytes 8355840 | tf_op jit(solution)/shard_map/slice | solution.py:70
  23.0 1.4 fusion.61
  24.4 0.8 constant_dynamic-update-slice_fusion
  25.2 1.9 %bitcast_dynamic-update-slice_fusion.2 = f32[5,16,32,256]{3,2,1,0:T(8,128)} fusion(f32[5,16,32,256]{3,2,1,0:T(8,128)} %constant_dynamic-update-slice_fusion, f32[16,32,256]{2,1,0:T(8,128)} %param.10), kind=kLoop, calls=%fused_computation.80 | loop fusion | bytes 1048576
  27.1 1.9 %bitcast_dynamic-update-slice_fusion.1 = f32[5,16,32,256]{3,2,1,0:T(8,128)} fusion(f32[5,16,32,256]{3,2,1,0:T(8,128)} %bitcast_dynamic-update-slice_fusion.2, f32[16,32,256]{2,1,0:T(8,128)} %param.12), kind=kLoop, calls=%fused_computation.79 | loop fusion | bytes 1048576
  29.0 1.9 %bitcast_dynamic-update-slice_fusion = f32[5,16,32,256]{3,2,1,0:T(8,128)} fusion(f32[5,16,32,256]{3,2,1,0:T(8,128)} %bitcast_dynamic-update-slice_fusion.1, f32[16,32,256]{2,1,0:T(8,128)} %param.13, s32[32,256]{1,0:T(8,128)S(1)} %copy-done.6), kind=kLoop, calls=%fused_computation.78 | loop fusion | flops 262144 | bytes 1081344 | tf_op jit(solution)/shard_map/stack | solution.py:36
  31.0 2.2 %fusion = f32[5,16,34,256]{3,2,1,0:T(8,128)S(1)} fusion(f32[2,16,1,256]{3,2,1,0:T(1,128)S(1)} %collective-permute-done, f32[5,16,32,256]{3,2,1,0:T(8,128)} %bitcast_dynamic-update-slice_fusion, f32[34]{0:T(128)S(1)} %pad.44.clone), kind=kLoop, calls=%fused_computation.1 | loop fusion | flops 2785280 | bytes 5439624 | tf_op jit(solution)/shard_map/concatenate | solution.py:43
  33.2 0.3 slice_bitcast_fusion
  33.5 0.2 pad_slice_fusion
  33.9 1.1 copy-done.2
  35.1 0.7 copy-done.1
  35.8 0.3 copy-done.3
  36.0 1.9 %fusion.29 = f32[4,16,32,256]{3,2,1,0:T(8,128)S(1)} fusion(f32[4,16,32,256]{3,2,1,0:T(8,128)S(1)} %copy-done, f32[4,16,1,256]{3,2,1,0:T(1,128)S(1)} %collective-permute-done.2, f32[4,16,1,256]{3,2,1,0:T(1,128)S(1)} %collective-permute-done.1, f32[4,16,32,1]{3,2,1,0:T(8,128)S(1)} %copy-done.3, f32[4,16,32,255]{3,2,1,0:T(8,128)S(1)} %copy-done.2, ...), kind=kLoop, calls=%fused_computation.38 | loop fusion | flops 8388608 | bytes 10616832 | tf_op jit(solution)/shard_map/add | solution.py:72
  37.9 0.2 slice.258
  38.2 0.7 fusion.36
  38.9 0.8 fusion.59
  39.9 7.5 %collective-permute-start.3 = (f32[4,16,1,256]{3,2,1,0:T(1,128)S(1)}, f32[4,16,1,256]{3,2,1,0:T(1,128)S(1)}, u32[]{:S(2)}, u32[]{:S(2)}) collective-permute-start(f32[4,16,1,256]{3,2,1,0:T(1,128)S(1)} %get-tuple-element.23), channel_id=1, source_target_pairs={{16,0},{32,16},{48,32},{64,48},{80,64},{96,80},{112,96},{128,112},... | collective-permute-start | bytes 196616 | tf_op jit(solution)/shard_map/ppermute | solution.py:23
  47.4 1.9 %collective-permute-start.4 = (f32[4,16,1,256]{3,2,1,0:T(1,128)S(1)}, f32[4,16,1,256]{3,2,1,0:T(1,128)S(1)}, u32[]{:S(2)}, u32[]{:S(2)}) collective-permute-start(f32[4,16,1,256]{3,2,1,0:T(1,128)S(1)} %get-tuple-element.24), channel_id=1, source_target_pairs={{0,16},{16,32},{32,48},{48,64},{64,80},{80,96},{96,112},{112,128},... | collective-permute-start | bytes 196616 | tf_op jit(solution)/shard_map/ppermute | solution.py:21
  49.3 0.4 fusion.58
  49.7 7.5 %collective-permute-done.4 = f32[4,16,1,256]{3,2,1,0:T(1,128)S(1)} collective-permute-done((f32[4,16,1,256]{3,2,1,0:T(1,128)S(1)}, f32[4,16,1,256]{3,2,1,0:T(1,128)S(1)}, u32[]{:S(2)}, u32[]{:S(2)}) %collective-permute-start.4) | collective-permute-done | bytes 65568 | tf_op jit(solution)/shard_map/ppermute | solution.py:21
  57.2 2.0 %fusion.21 = f32[4,16,32,256]{3,2,1,0:T(8,128)S(1)} fusion(f32[4,16,32,256]{3,2,1,0:T(8,128)S(1)} %fusion.36, f32[4,16,1,256]{3,2,1,0:T(1,128)S(1)} %collective-permute-done.4, f32[4,16,1,256]{3,2,1,0:T(1,128)S(1)} %collective-permute-done.3, f32[4,16,32,1]{3,2,1,0:T(8,128)S(1)} %get-tuple-element.20, f32[4,16,32,255]{3,2,1,0:T(8,128)S(1)} %get-tuple-element.22, ...), kind=kLoop, calls=%fused_computation.28 | loop fusion | flops 8388608 | bytes 10616832 | tf_op jit(solution)/shard_map/add | solution.py:72
  59.2 0.2 slice.266
  59.5 0.7 fusion.40
  60.2 0.8 fusion.56
  61.1 1.9 %collective-permute-start.5 = (f32[4,16,1,256]{3,2,1,0:T(1,128)S(1)}, f32[4,16,1,256]{3,2,1,0:T(1,128)S(1)}, u32[]{:S(2)}, u32[]{:S(2)}) collective-permute-start(f32[4,16,1,256]{3,2,1,0:T(1,128)S(1)} %get-tuple-element.17), channel_id=1, source_target_pairs={{16,0},{32,16},{48,32},{64,48},{80,64},{96,80},{112,96},{128,112},... | collective-permute-start | bytes 196616 | tf_op jit(solution)/shard_map/ppermute | solution.py:23
  63.1 3.9 %collective-permute-start.6 = (f32[4,16,1,256]{3,2,1,0:T(1,128)S(1)}, f32[4,16,1,256]{3,2,1,0:T(1,128)S(1)}, u32[]{:S(2)}, u32[]{:S(2)}) collective-permute-start(f32[4,16,1,256]{3,2,1,0:T(1,128)S(1)} %get-tuple-element.18), channel_id=1, source_target_pairs={{0,16},{16,32},{32,48},{48,64},{64,80},{80,96},{96,112},{112,128},... | collective-permute-start | bytes 196616 | tf_op jit(solution)/shard_map/ppermute | solution.py:21
  67.0 0.4 fusion.55
  67.4 5.5 %collective-permute-done.6 = f32[4,16,1,256]{3,2,1,0:T(1,128)S(1)} collective-permute-done((f32[4,16,1,256]{3,2,1,0:T(1,128)S(1)}, f32[4,16,1,256]{3,2,1,0:T(1,128)S(1)}, u32[]{:S(2)}, u32[]{:S(2)}) %collective-permute-start.6) | collective-permute-done | bytes 65568 | tf_op jit(solution)/shard_map/ppermute | solution.py:21
  72.8 2.0 %fusion.13 = f32[4,16,32,256]{3,2,1,0:T(8,128)S(1)} fusion(f32[4,16,32,256]{3,2,1,0:T(8,128)S(1)} %fusion.40, f32[4,16,1,256]{3,2,1,0:T(1,128)S(1)} %collective-permute-done.6, f32[4,16,1,256]{3,2,1,0:T(1,128)S(1)} %collective-permute-done.5, f32[4,16,32,1]{3,2,1,0:T(8,128)S(1)} %get-tuple-element.14, f32[4,16,32,255]{3,2,1,0:T(8,128)S(1)} %get-tuple-element.16, ...), kind=kLoop, calls=%fused_computation.18 | loop fusion | flops 8388608 | bytes 10616832 | tf_op jit(solution)/shard_map/add | solution.py:72
  74.9 0.2 slice.274
  75.1 0.6 fusion.44
  75.7 0.8 fusion.53
  76.5 0.1 fusion.54
  76.6 1.9 %collective-permute-start.7 = (f32[4,16,1,256]{3,2,1,0:T(1,128)S(1)}, f32[4,16,1,256]{3,2,1,0:T(1,128)S(1)}, u32[]{:S(2)}, u32[]{:S(2)}) collective-permute-start(f32[4,16,1,256]{3,2,1,0:T(1,128)S(1)} %get-tuple-element.11), channel_id=1, source_target_pairs={{16,0},{32,16},{48,32},{64,48},{80,64},{96,80},{112,96},{128,112},... | collective-permute-start | bytes 196616 | tf_op jit(solution)/shard_map/ppermute | solution.py:23
  78.6 3.9 %collective-permute-start.8 = (f32[4,16,1,256]{3,2,1,0:T(1,128)S(1)}, f32[4,16,1,256]{3,2,1,0:T(1,128)S(1)}, u32[]{:S(2)}, u32[]{:S(2)}) collective-permute-start(f32[4,16,1,256]{3,2,1,0:T(1,128)S(1)} %get-tuple-element.12), channel_id=1, source_target_pairs={{0,16},{16,32},{32,48},{48,64},{64,80},{80,96},{96,112},{112,128},... | collective-permute-start | bytes 196616 | tf_op jit(solution)/shard_map/ppermute | solution.py:21
  82.5 0.4 fusion.52
  82.9 5.5 %collective-permute-done.8 = f32[4,16,1,256]{3,2,1,0:T(1,128)S(1)} collective-permute-done((f32[4,16,1,256]{3,2,1,0:T(1,128)S(1)}, f32[4,16,1,256]{3,2,1,0:T(1,128)S(1)}, u32[]{:S(2)}, u32[]{:S(2)}) %collective-permute-start.8) | collective-permute-done | bytes 65568 | tf_op jit(solution)/shard_map/ppermute | solution.py:21
  88.3 2.0 %fusion.5 = f32[4,16,32,256]{3,2,1,0:T(8,128)S(1)} fusion(f32[4,16,32,256]{3,2,1,0:T(8,128)S(1)} %fusion.44, f32[4,16,1,256]{3,2,1,0:T(1,128)S(1)} %collective-permute-done.8, f32[4,16,1,256]{3,2,1,0:T(1,128)S(1)} %collective-permute-done.7, f32[4,16,32,1]{3,2,1,0:T(8,128)S(1)} %get-tuple-element.8, f32[4,16,32,255]{3,2,1,0:T(8,128)S(1)} %get-tuple-element.10, ...), kind=kLoop, calls=%fused_computation.8 | loop fusion | flops 8388608 | bytes 10616832 | tf_op jit(solution)/shard_map/add | solution.py:72
  90.4 0.2 slice.282
  90.6 0.5 fusion.48
  91.2 0.2 copy-done.7
  91.5 54.3 %psum.7 = f32[32,256]{1,0:T(8,128)} all-reduce(f32[32,256]{1,0:T(8,128)S(1)} %fusion.51), channel_id=1, replica_groups=mesh['dom'=32,'grp'=16] {'grp'}, use_global_device_ids=true, to_apply=%region_1.0 | all-reduce | flops 8192 | bytes 65536 | tf_op jit(solution)/shard_map/psum | solution.py:85
  (31 shorter events, 0.6 us)
Async XLA Ops:
  0.6 19.6 %copy-start = (f32[4,16,32,256]{3,2,1,0:T(8,128)S(1)}, f32[4,16,32,256]{3,2,1,0:T(8,128)}, u32[]{:S(2)}) copy-start(f32[4,16,32,256]{3,2,1,0:T(8,128)} %param.8) | copy-start | bytes 6291460
  1.8 29.2 %collective-permute-start = (f32[2,16,1,256]{3,2,1,0:T(1,128)S(1)}, f32[2,16,1,256]{3,2,1,0:T(1,128)S(1)}, u32[]{:S(2)}, u32[]{:S(2)}) collective-permute-start(f32[2,16,1,256]{3,2,1,0:T(1,128)S(1)} %pad_maximum_fusion.8), channel_id=1, source_target_pairs={{0,16},{16,32},{32,48},{48,64},{64,80},{80,96},{96,112},{112,128},... | collective-permute-start | bytes 98312 | tf_op jit(solution)/shard_map/ppermute | solution.py:11
  6.9 27.0 %collective-permute-start.1 = (f32[4,16,1,256]{3,2,1,0:T(1,128)S(1)}, f32[4,16,1,256]{3,2,1,0:T(1,128)S(1)}, u32[]{:S(2)}, u32[]{:S(2)}) collective-permute-start(f32[4,16,1,256]{3,2,1,0:T(1,128)S(1)} %get-tuple-element.29), channel_id=1, source_target_pairs={{16,0},{32,16},{48,32},{64,48},{80,64},{96,80},{112,96},{128,112},... | collective-permute-start | bytes 196616 | tf_op jit(solution)/shard_map/ppermute | solution.py:23
  16.4 17.6 %collective-permute-start.2 = (f32[4,16,1,256]{3,2,1,0:T(1,128)S(1)}, f32[4,16,1,256]{3,2,1,0:T(1,128)S(1)}, u32[]{:S(2)}, u32[]{:S(2)}) collective-permute-start(f32[4,16,1,256]{3,2,1,0:T(1,128)S(1)} %get-tuple-element.30), channel_id=1, source_target_pairs={{0,16},{16,32},{32,48},{48,64},{64,80},{80,96},{96,112},{112,128},... | collective-permute-start | bytes 196616 | tf_op jit(solution)/shard_map/ppermute | solution.py:21
  23.0 1.4 copy-start.5
  24.4 4.6 %copy-start.6 = (s32[32,256]{1,0:T(8,128)S(1)}, s32[32,256]{1,0:T(8,128)}, u32[]{:S(2)}) copy-start(s32[32,256]{1,0:T(8,128)} %param.15) | copy-start | bytes 98308
  33.5 1.6 %copy-start.2 = (f32[4,16,32,255]{3,2,1,0:T(8,128)S(1)}, f32[4,16,32,255]{3,2,1,0:T(8,128)}, u32[]{:S(2)}) copy-start(f32[4,16,32,255]{3,2,1,0:T(8,128)} %get-tuple-element.28) | copy-start | bytes 6266884
  33.7 2.1 %copy-start.1 = (f32[4,16,32,255]{3,2,1,0:T(8,128)S(1)}, f32[4,16,32,255]{3,2,1,0:T(8,128)}, u32[]{:S(2)}) copy-start(f32[4,16,32,255]{3,2,1,0:T(8,128)} %get-tuple-element.27) | copy-start | bytes 6266884
  33.7 2.3 %copy-start.3 = (f32[4,16,32,1]{3,2,1,0:T(8,128)S(1)}, f32[4,16,32,1]{3,2,1,0:T(8,128)}, u32[]{:S(2)}) copy-start(f32[4,16,32,1]{3,2,1,0:T(8,128)} %get-tuple-element.26) | copy-start | bytes 24580
  39.9 9.9 %collective-permute-start.3 = (f32[4,16,1,256]{3,2,1,0:T(1,128)S(1)}, f32[4,16,1,256]{3,2,1,0:T(1,128)S(1)}, u32[]{:S(2)}, u32[]{:S(2)}) collective-permute-start(f32[4,16,1,256]{3,2,1,0:T(1,128)S(1)} %get-tuple-element.23), channel_id=1, source_target_pairs={{16,0},{32,16},{48,32},{64,48},{80,64},{96,80},{112,96},{128,112},... | collective-permute-start | bytes 196616 | tf_op jit(solution)/shard_map/ppermute | solution.py:23
  47.4 9.8 %collective-permute-start.4 = (f32[4,16,1,256]{3,2,1,0:T(1,128)S(1)}, f32[4,16,1,256]{3,2,1,0:T(1,128)S(1)}, u32[]{:S(2)}, u32[]{:S(2)}) collective-permute-start(f32[4,16,1,256]{3,2,1,0:T(1,128)S(1)} %get-tuple-element.24), channel_id=1, source_target_pairs={{0,16},{16,32},{32,48},{48,64},{64,80},{80,96},{96,112},{112,128},... | collective-permute-start | bytes 196616 | tf_op jit(solution)/shard_map/ppermute | solution.py:21
  61.1 6.2 %collective-permute-start.5 = (f32[4,16,1,256]{3,2,1,0:T(1,128)S(1)}, f32[4,16,1,256]{3,2,1,0:T(1,128)S(1)}, u32[]{:S(2)}, u32[]{:S(2)}) collective-permute-start(f32[4,16,1,256]{3,2,1,0:T(1,128)S(1)} %get-tuple-element.17), channel_id=1, source_target_pairs={{16,0},{32,16},{48,32},{64,48},{80,64},{96,80},{112,96},{128,112},... | collective-permute-start | bytes 196616 | tf_op jit(solution)/shard_map/ppermute | solution.py:23
  63.1 9.8 %collective-permute-start.6 = (f32[4,16,1,256]{3,2,1,0:T(1,128)S(1)}, f32[4,16,1,256]{3,2,1,0:T(1,128)S(1)}, u32[]{:S(2)}, u32[]{:S(2)}) collective-permute-start(f32[4,16,1,256]{3,2,1,0:T(1,128)S(1)} %get-tuple-element.18), channel_id=1, source_target_pairs={{0,16},{16,32},{32,48},{48,64},{64,80},{80,96},{96,112},{112,128},... | collective-permute-start | bytes 196616 | tf_op jit(solution)/shard_map/ppermute | solution.py:21
  76.6 6.2 %collective-permute-start.7 = (f32[4,16,1,256]{3,2,1,0:T(1,128)S(1)}, f32[4,16,1,256]{3,2,1,0:T(1,128)S(1)}, u32[]{:S(2)}, u32[]{:S(2)}) collective-permute-start(f32[4,16,1,256]{3,2,1,0:T(1,128)S(1)} %get-tuple-element.11), channel_id=1, source_target_pairs={{16,0},{32,16},{48,32},{64,48},{80,64},{96,80},{112,96},{128,112},... | collective-permute-start | bytes 196616 | tf_op jit(solution)/shard_map/ppermute | solution.py:23
  78.6 9.8 %collective-permute-start.8 = (f32[4,16,1,256]{3,2,1,0:T(1,128)S(1)}, f32[4,16,1,256]{3,2,1,0:T(1,128)S(1)}, u32[]{:S(2)}, u32[]{:S(2)}) collective-permute-start(f32[4,16,1,256]{3,2,1,0:T(1,128)S(1)} %get-tuple-element.12), channel_id=1, source_target_pairs={{0,16},{16,32},{32,48},{48,64},{64,80},{80,96},{96,112},{112,128},... | collective-permute-start | bytes 196616 | tf_op jit(solution)/shard_map/ppermute | solution.py:21
  90.6 0.8 copy-start.7
  91.4 54.3 %copy-start.4 = (f32[4,16,32,256]{3,2,1,0:T(8,128)}, f32[4,16,32,256]{3,2,1,0:T(8,128)S(1)}, u32[]{:S(2)}) copy-start(f32[4,16,32,256]{3,2,1,0:T(8,128)S(1)} %fusion.48) | copy-start | bytes 6291460
where the time goes:
time: 146 us
  blocking collectives  54.3 us (37%)
  starting transfers between devices  36.3 us (25%)
  local copies, waits for them, and re-layouts  19.3 us (13%)
  waiting for transfers between devices  18.4 us (13%)
  other arithmetic  16.4 us (11%)
    psum x1, blocking collectives, local(): flux_gradient = lax.psum(local_grad, 'grp')  54.3 us
    ppermute x4, starting transfers between devices, with_halo(): lax.ppermute(head, axis, [((i + 1) % count, i) for i in range(count)])  20.8 us
    ppermute x4, waiting for transfers between devices, with_halo(): lax.ppermute(tail, axis, [(i, (i + 1) % count) for i in range(count)])  18.4 us
    ppermute x4, starting transfers between devices, with_halo(): lax.ppermute(tail, axis, [(i, (i + 1) % count) for i in range(count)])  11.7 us
    unnamed x20, local copies, waits for them, and re-layouts  8.83 us
    add x4, other arithmetic, local(): center + coef_e * (east - center) + coef_w * (west - center)  8 us
    slice x8, local copies, waits for them, and re-layouts, local(): south = jnp.concatenate([center[..., :1], center[..., :-1]], axis=-1)  7.72 us
    ppermute x1, starting transfers between devices, passed_along(): lax.ppermute(value, axis, [(i, (i + by) % size) for i in range(size)])  3.83 us
  transfers between devices with their start and end apart: 9, of which 3 were waited for; matrix products, arithmetic and copies ran while one was open for 12% of the time, Pallas kernels for 0%

commit v1 on v0

--- a/solution.py
+++ b/solution.py
@@ -82,7 +82,8 @@
     tag_ids = lax.axis_index("grp") * tags + lax.broadcasted_iota(jnp.int32, (tags, cols, lats), 0)
     select = (region_map[None] == tag_ids).astype(jnp.float32)
     local_grad = jnp.sum(select * accum, axis=0)
-    flux_gradient = lax.psum(local_grad, "grp")
+    parts = lax.all_gather(local_grad, "grp")
+    flux_gradient = jnp.sum(parts, axis=0)
     return (lam, flux_gradient)
 
 

time: 146 us -> 118 us (0.81)
  the two profiles are of different devices: /device:TPU:4 before, /device:TPU:1 now
where the time goes in v1:
time: 118 us; the launch traced here: 117 us
  starting transfers between devices  37.7 us (32%)
  blocking collectives  26.1 us (22%)
  local copies, waits for them, and re-layouts  19.3 us (16%)
  other arithmetic  17 us (14%)
  waiting for transfers between devices  16.1 us (14%)
    all_gather x1, blocking collectives, local(): parts = lax.all_gather(local_grad, 'grp')  26.1 us
    ppermute x4, starting transfers between devices, with_halo(): lax.ppermute(head, axis, [((i + 1) % count, i) for i in range(count)])  22.8 us
    ppermute x4, waiting for transfers between devices, with_halo(): lax.ppermute(tail, axis, [(i, (i + 1) % count) for i in range(count)])  16 us
    ppermute x4, starting transfers between devices, with_halo(): lax.ppermute(tail, axis, [(i, (i + 1) % count) for i in range(count)])  10.6 us
    unnamed x20, local copies, waits for them, and re-layouts  8.83 us
    add x4, other arithmetic, local(): center + coef_e * (east - center) + coef_w * (west - center)  8 us
    slice x8, local copies, waits for them, and re-layouts, local(): south = jnp.concatenate([center[..., :1], center[..., :-1]], axis=-1)  7.72 us
    ppermute x1, starting transfers between devices, passed_along(): lax.ppermute(value, axis, [(i, (i + by) % size) for i in range(size)])  4.38 us
  transfers between devices with their start and end apart: 9, of which 3 were waited for; matrix products, arithmetic and copies ran while one was open for 15% of the time, Pallas kernels for 0%

profile of v1, /device:TPU:1, one launch (start us, length us, event | category | flops | bytes accessed | tf_op | source)
XLA Modules:
  0.0 117.3 jit_solution(10715594087810283664)
XLA Ops:
  0.6 1.2 pad_maximum_fusion.8
  1.8 4.4 %collective-permute-start = (f32[2,16,1,256]{3,2,1,0:T(1,128)S(1)}, f32[2,16,1,256]{3,2,1,0:T(1,128)S(1)}, u32[]{:S(2)}, u32[]{:S(2)}) collective-permute-start(f32[2,16,1,256]{3,2,1,0:T(1,128)S(1)} %pad_maximum_fusion.8), channel_id=1, source_target_pairs={{0,16},{16,32},{32,48},{48,64},{64,80},{80,96},{96,112},{112,128},... | collective-permute-start | bytes 98312 | tf_op jit(solution)/shard_map/ppermute | solution.py:11
  6.2 1.3 %fusion.63 = (f32[4,16,1,256]{3,2,1,0:T(1,128)S(1)}, f32[4,16,1,256]{3,2,1,0:T(1,128)S(1)}) fusion(f32[4,16,32,256]{3,2,1,0:T(8,128)} %param.8), kind=kLoop, calls=%fused_computation.104 | loop fusion | bytes 262144 | tf_op jit(solution)/shard_map/slice | solution.py:17
  7.5 12.0 %collective-permute-start.1 = (f32[4,16,1,256]{3,2,1,0:T(1,128)S(1)}, f32[4,16,1,256]{3,2,1,0:T(1,128)S(1)}, u32[]{:S(2)}, u32[]{:S(2)}) collective-permute-start(f32[4,16,1,256]{3,2,1,0:T(1,128)S(1)} %get-tuple-element.29), channel_id=1, source_target_pairs={{16,0},{32,16},{48,32},{64,48},{80,64},{96,80},{112,96},{128,112},... | collective-permute-start | bytes 196616 | tf_op jit(solution)/shard_map/ppermute | solution.py:23
  19.4 1.9 %collective-permute-start.2 = (f32[4,16,1,256]{3,2,1,0:T(1,128)S(1)}, f32[4,16,1,256]{3,2,1,0:T(1,128)S(1)}, u32[]{:S(2)}, u32[]{:S(2)}) collective-permute-start(f32[4,16,1,256]{3,2,1,0:T(1,128)S(1)} %get-tuple-element.30), channel_id=1, source_target_pairs={{0,16},{16,32},{32,48},{48,64},{64,80},{80,96},{96,112},{112,128},... | collective-permute-start | bytes 196616 | tf_op jit(solution)/shard_map/ppermute | solution.py:21
  21.4 1.9 %constant_dynamic-update-slice_fusion.1 = f32[5,16,32,256]{3,2,1,0:T(8,128)} fusion(f32[16,32,256]{2,1,0:T(8,128)} %param.9), kind=kLoop, calls=%fused_computation.90 | loop fusion | bytes 1048576
  23.3 2.8 %fusion.62 = (f32[4,16,32,255]{3,2,1,0:T(8,128)}, f32[4,16,32,255]{3,2,1,0:T(8,128)}) fusion(f32[4,16,32,256]{3,2,1,0:T(8,128)S(1)} %copy-done), kind=kLoop, calls=%fused_computation.103 | loop fusion | bytes 8355840 | tf_op jit(solution)/shard_map/slice | solution.py:70
  26.0 1.4 %fusion.61 = (f32[4,16,32,1]{3,2,1,0:T(8,128)S(1)}, f32[4,16,32,1]{3,2,1,0:T(8,128)}) fusion(f32[4,16,32,256]{3,2,1,0:T(8,128)S(1)} %copy-done), kind=kLoop, calls=%fused_computation.102 | loop fusion | bytes 32768 | tf_op jit(solution)/shard_map/slice | solution.py:70
  27.4 0.8 constant_dynamic-update-slice_fusion
  28.3 1.9 %bitcast_dynamic-update-slice_fusion.2 = f32[5,16,32,256]{3,2,1,0:T(8,128)} fusion(f32[5,16,32,256]{3,2,1,0:T(8,128)} %constant_dynamic-update-slice_fusion, f32[16,32,256]{2,1,0:T(8,128)} %param.10), kind=kLoop, calls=%fused_computation.80 | loop fusion | bytes 1048576
  30.2 1.9 %bitcast_dynamic-update-slice_fusion.1 = f32[5,16,32,256]{3,2,1,0:T(8,128)} fusion(f32[5,16,32,256]{3,2,1,0:T(8,128)} %bitcast_dynamic-update-slice_fusion.2, f32[16,32,256]{2,1,0:T(8,128)} %param.12), kind=kLoop, calls=%fused_computation.79 | loop fusion | bytes 1048576
  32.0 1.9 %bitcast_dynamic-update-slice_fusion = f32[5,16,32,256]{3,2,1,0:T(8,128)} fusion(f32[5,16,32,256]{3,2,1,0:T(8,128)} %bitcast_dynamic-update-slice_fusion.1, f32[16,32,256]{2,1,0:T(8,128)} %param.13, s32[32,256]{1,0:T(8,128)S(1)} %copy-done.6), kind=kLoop, calls=%fused_computation.78 | loop fusion | flops 262144 | bytes 1081344 | tf_op jit(solution)/shard_map/stack | solution.py:36
  34.0 2.2 %fusion = f32[5,16,34,256]{3,2,1,0:T(8,128)S(1)} fusion(f32[2,16,1,256]{3,2,1,0:T(1,128)S(1)} %collective-permute-done, f32[5,16,32,256]{3,2,1,0:T(8,128)} %bitcast_dynamic-update-slice_fusion, f32[34]{0:T(128)S(1)} %pad.44.clone), kind=kLoop, calls=%fused_computation.1 | loop fusion | flops 2785280 | bytes 5439624 | tf_op jit(solution)/shard_map/concatenate | solution.py:43
  36.2 0.3 slice_bitcast_fusion
  36.6 0.2 pad_slice_fusion
  37.0 1.1 copy-done.2
  38.1 0.7 copy-done.1
  38.8 0.3 copy-done.3
  39.1 1.9 %fusion.29 = f32[4,16,32,256]{3,2,1,0:T(8,128)S(1)} fusion(f32[4,16,32,256]{3,2,1,0:T(8,128)S(1)} %copy-done, f32[4,16,1,256]{3,2,1,0:T(1,128)S(1)} %collective-permute-done.2, f32[4,16,1,256]{3,2,1,0:T(1,128)S(1)} %collective-permute-done.1, f32[4,16,32,1]{3,2,1,0:T(8,128)S(1)} %copy-done.3, f32[4,16,32,255]{3,2,1,0:T(8,128)S(1)} %copy-done.2, ...), kind=kLoop, calls=%fused_computation.38 | loop fusion | flops 8388608 | bytes 10616832 | tf_op jit(solution)/shard_map/add | solution.py:72
  41.0 0.2 slice.258
  41.3 0.7 fusion.36
  42.0 0.8 fusion.59
  42.9 7.0 %collective-permute-start.3 = (f32[4,16,1,256]{3,2,1,0:T(1,128)S(1)}, f32[4,16,1,256]{3,2,1,0:T(1,128)S(1)}, u32[]{:S(2)}, u32[]{:S(2)}) collective-permute-start(f32[4,16,1,256]{3,2,1,0:T(1,128)S(1)} %get-tuple-element.23), channel_id=1, source_target_pairs={{16,0},{32,16},{48,32},{64,48},{80,64},{96,80},{112,96},{128,112},... | collective-permute-start | bytes 196616 | tf_op jit(solution)/shard_map/ppermute | solution.py:23
  49.9 1.9 %collective-permute-start.4 = (f32[4,16,1,256]{3,2,1,0:T(1,128)S(1)}, f32[4,16,1,256]{3,2,1,0:T(1,128)S(1)}, u32[]{:S(2)}, u32[]{:S(2)}) collective-permute-start(f32[4,16,1,256]{3,2,1,0:T(1,128)S(1)} %get-tuple-element.24), channel_id=1, source_target_pairs={{0,16},{16,32},{32,48},{48,64},{64,80},{80,96},{96,112},{112,128},... | collective-permute-start | bytes 196616 | tf_op jit(solution)/shard_map/ppermute | solution.py:21
  51.8 0.4 fusion.58
  52.2 6.3 %collective-permute-done.4 = f32[4,16,1,256]{3,2,1,0:T(1,128)S(1)} collective-permute-done((f32[4,16,1,256]{3,2,1,0:T(1,128)S(1)}, f32[4,16,1,256]{3,2,1,0:T(1,128)S(1)}, u32[]{:S(2)}, u32[]{:S(2)}) %collective-permute-start.4) | collective-permute-done | bytes 65568 | tf_op jit(solution)/shard_map/ppermute | solution.py:21
  58.5 2.0 %fusion.21 = f32[4,16,32,256]{3,2,1,0:T(8,128)S(1)} fusion(f32[4,16,32,256]{3,2,1,0:T(8,128)S(1)} %fusion.36, f32[4,16,1,256]{3,2,1,0:T(1,128)S(1)} %collective-permute-done.4, f32[4,16,1,256]{3,2,1,0:T(1,128)S(1)} %collective-permute-done.3, f32[4,16,32,1]{3,2,1,0:T(8,128)S(1)} %get-tuple-element.20, f32[4,16,32,255]{3,2,1,0:T(8,128)S(1)} %get-tuple-element.22, ...), kind=kLoop, calls=%fused_computation.28 | loop fusion | flops 8388608 | bytes 10616832 | tf_op jit(solution)/shard_map/add | solution.py:72
  60.6 0.2 slice.266
  60.8 0.7 fusion.40
  61.5 0.8 fusion.56
  62.5 1.9 %collective-permute-start.5 = (f32[4,16,1,256]{3,2,1,0:T(1,128)S(1)}, f32[4,16,1,256]{3,2,1,0:T(1,128)S(1)}, u32[]{:S(2)}, u32[]{:S(2)}) collective-permute-start(f32[4,16,1,256]{3,2,1,0:T(1,128)S(1)} %get-tuple-element.17), channel_id=1, source_target_pairs={{16,0},{32,16},{48,32},{64,48},{80,64},{96,80},{112,96},{128,112},... | collective-permute-start | bytes 196616 | tf_op jit(solution)/shard_map/ppermute | solution.py:23
  64.4 3.4 %collective-permute-start.6 = (f32[4,16,1,256]{3,2,1,0:T(1,128)S(1)}, f32[4,16,1,256]{3,2,1,0:T(1,128)S(1)}, u32[]{:S(2)}, u32[]{:S(2)}) collective-permute-start(f32[4,16,1,256]{3,2,1,0:T(1,128)S(1)} %get-tuple-element.18), channel_id=1, source_target_pairs={{0,16},{16,32},{32,48},{48,64},{64,80},{80,96},{96,112},{112,128},... | collective-permute-start | bytes 196616 | tf_op jit(solution)/shard_map/ppermute | solution.py:21
  67.8 0.4 fusion.55
  68.2 4.9 %collective-permute-done.6 = f32[4,16,1,256]{3,2,1,0:T(1,128)S(1)} collective-permute-done((f32[4,16,1,256]{3,2,1,0:T(1,128)S(1)}, f32[4,16,1,256]{3,2,1,0:T(1,128)S(1)}, u32[]{:S(2)}, u32[]{:S(2)}) %collective-permute-start.6) | collective-permute-done | bytes 65568 | tf_op jit(solution)/shard_map/ppermute | solution.py:21
  73.0 2.0 %fusion.13 = f32[4,16,32,256]{3,2,1,0:T(8,128)S(1)} fusion(f32[4,16,32,256]{3,2,1,0:T(8,128)S(1)} %fusion.40, f32[4,16,1,256]{3,2,1,0:T(1,128)S(1)} %collective-permute-done.6, f32[4,16,1,256]{3,2,1,0:T(1,128)S(1)} %collective-permute-done.5, f32[4,16,32,1]{3,2,1,0:T(8,128)S(1)} %get-tuple-element.14, f32[4,16,32,255]{3,2,1,0:T(8,128)S(1)} %get-tuple-element.16, ...), kind=kLoop, calls=%fused_computation.18 | loop fusion | flops 8388608 | bytes 10616832 | tf_op jit(solution)/shard_map/add | solution.py:72
  75.1 0.2 slice.274
  75.3 0.6 fusion.44
  75.9 0.8 fusion.53
  76.8 1.9 %collective-permute-start.7 = (f32[4,16,1,256]{3,2,1,0:T(1,128)S(1)}, f32[4,16,1,256]{3,2,1,0:T(1,128)S(1)}, u32[]{:S(2)}, u32[]{:S(2)}) collective-permute-start(f32[4,16,1,256]{3,2,1,0:T(1,128)S(1)} %get-tuple-element.11), channel_id=1, source_target_pairs={{16,0},{32,16},{48,32},{64,48},{80,64},{96,80},{112,96},{128,112},... | collective-permute-start | bytes 196616 | tf_op jit(solution)/shard_map/ppermute | solution.py:23
  78.8 3.4 %collective-permute-start.8 = (f32[4,16,1,256]{3,2,1,0:T(1,128)S(1)}, f32[4,16,1,256]{3,2,1,0:T(1,128)S(1)}, u32[]{:S(2)}, u32[]{:S(2)}) collective-permute-start(f32[4,16,1,256]{3,2,1,0:T(1,128)S(1)} %get-tuple-element.12), channel_id=1, source_target_pairs={{0,16},{16,32},{32,48},{48,64},{64,80},{80,96},{96,112},{112,128},... | collective-permute-start | bytes 196616 | tf_op jit(solution)/shard_map/ppermute | solution.py:21
  82.1 0.4 fusion.52
  82.5 4.9 %collective-permute-done.8 = f32[4,16,1,256]{3,2,1,0:T(1,128)S(1)} collective-permute-done((f32[4,16,1,256]{3,2,1,0:T(1,128)S(1)}, f32[4,16,1,256]{3,2,1,0:T(1,128)S(1)}, u32[]{:S(2)}, u32[]{:S(2)}) %collective-permute-start.8) | collective-permute-done | bytes 65568 | tf_op jit(solution)/shard_map/ppermute | solution.py:21
  87.4 2.0 %fusion.5 = f32[4,16,32,256]{3,2,1,0:T(8,128)S(1)} fusion(f32[4,16,32,256]{3,2,1,0:T(8,128)S(1)} %fusion.44, f32[4,16,1,256]{3,2,1,0:T(1,128)S(1)} %collective-permute-done.8, f32[4,16,1,256]{3,2,1,0:T(1,128)S(1)} %collective-permute-done.7, f32[4,16,32,1]{3,2,1,0:T(8,128)S(1)} %get-tuple-element.8, f32[4,16,32,255]{3,2,1,0:T(8,128)S(1)} %get-tuple-element.10, ...), kind=kLoop, calls=%fused_computation.8 | loop fusion | flops 8388608 | bytes 10616832 | tf_op jit(solution)/shard_map/add | solution.py:72
  89.4 0.2 slice.282
  89.7 0.5 fusion.48
  90.2 0.2 copy-done.7
  90.5 26.1 %all-gather = f32[512,256]{1,0:T(8,128)S(1)} all-gather(f32[32,256]{1,0:T(8,128)S(1)} %fusion.51), channel_id=2, replica_groups=mesh['dom'=32,'grp'=16] {'grp'}, dimensions={0}, use_global_device_ids=true | all-gather | bytes 557056 | tf_op jit(solution)/shard_map/all_gather | solution.py:85
  116.6 0.6 reduce_sum.19
  (32 shorter events, 0.7 us)
Async XLA Ops:
  0.6 22.6 %copy-start = (f32[4,16,32,256]{3,2,1,0:T(8,128)S(1)}, f32[4,16,32,256]{3,2,1,0:T(8,128)}, u32[]{:S(2)}) copy-start(f32[4,16,32,256]{3,2,1,0:T(8,128)} %param.8) | copy-start | bytes 6291460
  1.8 32.2 %collective-permute-start = (f32[2,16,1,256]{3,2,1,0:T(1,128)S(1)}, f32[2,16,1,256]{3,2,1,0:T(1,128)S(1)}, u32[]{:S(2)}, u32[]{:S(2)}) collective-permute-start(f32[2,16,1,256]{3,2,1,0:T(1,128)S(1)} %pad_maximum_fusion.8), channel_id=1, source_target_pairs={{0,16},{16,32},{32,48},{48,64},{64,80},{80,96},{96,112},{112,128},... | collective-permute-start | bytes 98312 | tf_op jit(solution)/shard_map/ppermute | solution.py:11
  7.5 29.5 %collective-permute-start.1 = (f32[4,16,1,256]{3,2,1,0:T(1,128)S(1)}, f32[4,16,1,256]{3,2,1,0:T(1,128)S(1)}, u32[]{:S(2)}, u32[]{:S(2)}) collective-permute-start(f32[4,16,1,256]{3,2,1,0:T(1,128)S(1)} %get-tuple-element.29), channel_id=1, source_target_pairs={{16,0},{32,16},{48,32},{64,48},{80,64},{96,80},{112,96},{128,112},... | collective-permute-start | bytes 196616 | tf_op jit(solution)/shard_map/ppermute | solution.py:23
  19.4 17.6 %collective-permute-start.2 = (f32[4,16,1,256]{3,2,1,0:T(1,128)S(1)}, f32[4,16,1,256]{3,2,1,0:T(1,128)S(1)}, u32[]{:S(2)}, u32[]{:S(2)}) collective-permute-start(f32[4,16,1,256]{3,2,1,0:T(1,128)S(1)} %get-tuple-element.30), channel_id=1, source_target_pairs={{0,16},{16,32},{32,48},{48,64},{64,80},{80,96},{96,112},{112,128},... | collective-permute-start | bytes 196616 | tf_op jit(solution)/shard_map/ppermute | solution.py:21
  26.0 1.4 %copy-start.5 = (f32[16,32,256]{2,1,0:T(8,128)S(1)}, f32[16,32,256]{2,1,0:T(8,128)}, u32[]{:S(2)}) copy-start(f32[16,32,256]{2,1,0:T(8,128)} %param.11) | copy-start | bytes 1572868
  27.4 4.6 %copy-start.6 = (s32[32,256]{1,0:T(8,128)S(1)}, s32[32,256]{1,0:T(8,128)}, u32[]{:S(2)}) copy-start(s32[32,256]{1,0:T(8,128)} %param.15) | copy-start | bytes 98308
  36.6 1.6 %copy-start.2 = (f32[4,16,32,255]{3,2,1,0:T(8,128)S(1)}, f32[4,16,32,255]{3,2,1,0:T(8,128)}, u32[]{:S(2)}) copy-start(f32[4,16,32,255]{3,2,1,0:T(8,128)} %get-tuple-element.28) | copy-start | bytes 6266884
  36.8 2.1 %copy-start.1 = (f32[4,16,32,255]{3,2,1,0:T(8,128)S(1)}, f32[4,16,32,255]{3,2,1,0:T(8,128)}, u32[]{:S(2)}) copy-start(f32[4,16,32,255]{3,2,1,0:T(8,128)} %get-tuple-element.27) | copy-start | bytes 6266884
  36.8 2.3 %copy-start.3 = (f32[4,16,32,1]{3,2,1,0:T(8,128)S(1)}, f32[4,16,32,1]{3,2,1,0:T(8,128)}, u32[]{:S(2)}) copy-start(f32[4,16,32,1]{3,2,1,0:T(8,128)} %get-tuple-element.26) | copy-start | bytes 24580
  42.9 9.3 %collective-permute-start.3 = (f32[4,16,1,256]{3,2,1,0:T(1,128)S(1)}, f32[4,16,1,256]{3,2,1,0:T(1,128)S(1)}, u32[]{:S(2)}, u32[]{:S(2)}) collective-permute-start(f32[4,16,1,256]{3,2,1,0:T(1,128)S(1)} %get-tuple-element.23), channel_id=1, source_target_pairs={{16,0},{32,16},{48,32},{64,48},{80,64},{96,80},{112,96},{128,112},... | collective-permute-start | bytes 196616 | tf_op jit(solution)/shard_map/ppermute | solution.py:23
  49.9 8.6 %collective-permute-start.4 = (f32[4,16,1,256]{3,2,1,0:T(1,128)S(1)}, f32[4,16,1,256]{3,2,1,0:T(1,128)S(1)}, u32[]{:S(2)}, u32[]{:S(2)}) collective-permute-start(f32[4,16,1,256]{3,2,1,0:T(1,128)S(1)} %get-tuple-element.24), channel_id=1, source_target_pairs={{0,16},{16,32},{32,48},{48,64},{64,80},{80,96},{96,112},{112,128},... | collective-permute-start | bytes 196616 | tf_op jit(solution)/shard_map/ppermute | solution.py:21
  62.5 5.7 %collective-permute-start.5 = (f32[4,16,1,256]{3,2,1,0:T(1,128)S(1)}, f32[4,16,1,256]{3,2,1,0:T(1,128)S(1)}, u32[]{:S(2)}, u32[]{:S(2)}) collective-permute-start(f32[4,16,1,256]{3,2,1,0:T(1,128)S(1)} %get-tuple-element.17), channel_id=1, source_target_pairs={{16,0},{32,16},{48,32},{64,48},{80,64},{96,80},{112,96},{128,112},... | collective-permute-start | bytes 196616 | tf_op jit(solution)/shard_map/ppermute | solution.py:23
  64.4 8.6 %collective-permute-start.6 = (f32[4,16,1,256]{3,2,1,0:T(1,128)S(1)}, f32[4,16,1,256]{3,2,1,0:T(1,128)S(1)}, u32[]{:S(2)}, u32[]{:S(2)}) collective-permute-start(f32[4,16,1,256]{3,2,1,0:T(1,128)S(1)} %get-tuple-element.18), channel_id=1, source_target_pairs={{0,16},{16,32},{32,48},{48,64},{64,80},{80,96},{96,112},{112,128},... | collective-permute-start | bytes 196616 | tf_op jit(solution)/shard_map/ppermute | solution.py:21
  76.8 5.7 %collective-permute-start.7 = (f32[4,16,1,256]{3,2,1,0:T(1,128)S(1)}, f32[4,16,1,256]{3,2,1,0:T(1,128)S(1)}, u32[]{:S(2)}, u32[]{:S(2)}) collective-permute-start(f32[4,16,1,256]{3,2,1,0:T(1,128)S(1)} %get-tuple-element.11), channel_id=1, source_target_pairs={{16,0},{32,16},{48,32},{64,48},{80,64},{96,80},{112,96},{128,112},... | collective-permute-start | bytes 196616 | tf_op jit(solution)/shard_map/ppermute | solution.py:23
  78.8 8.6 %collective-permute-start.8 = (f32[4,16,1,256]{3,2,1,0:T(1,128)S(1)}, f32[4,16,1,256]{3,2,1,0:T(1,128)S(1)}, u32[]{:S(2)}, u32[]{:S(2)}) collective-permute-start(f32[4,16,1,256]{3,2,1,0:T(1,128)S(1)} %get-tuple-element.12), channel_id=1, source_target_pairs={{0,16},{16,32},{32,48},{48,64},{64,80},{80,96},{96,112},{112,128},... | collective-permute-start | bytes 196616 | tf_op jit(solution)/shard_map/ppermute | solution.py:21
  89.7 0.8 copy-start.7
  90.4 26.8 %copy-start.4 = (f32[4,16,32,256]{3,2,1,0:T(8,128)}, f32[4,16,32,256]{3,2,1,0:T(8,128)S(1)}, u32[]{:S(2)}) copy-start(f32[4,16,32,256]{3,2,1,0:T(8,128)S(1)} %fusion.48) | copy-start | bytes 6291460
